TPU v7x, 32 devices: a whole 2x2x4 slice. The times are simulated.
32 devices in a mesh: tm: 8 (over z, x), clip: 4 (over y, core).
Axes of the slice: x: 2, y: 2, z: 4, core: 2. Of those that a mesh axis runs over, the one named last changes fastest.
Arguments:
- video: float32 [4, 8, 16, 32, 320], P('clip', 'tm'), may hold values from -6 to 6
- spatial_w: bfloat16 [9, 320, 320], P(None, 'clip'), may hold values from -0.109375 to 0.109375
- spatial_b: float32 [320], replicated, may hold values from -3 to 3
- temporal_w: float32 [3, 320, 320], P(None, 'clip'), may hold values from -0.1875 to 0.1875
- cotangent: float32 [4, 8, 16, 32, 320], P('clip', 'tm'), may hold values from -6 to 6
Outputs:
- output: float32 [4, 8, 16, 32, 320], P('clip', 'tm')
- grad_video: float32 [4, 8, 16, 32, 320], P('clip', 'tm')
- grad_temporal: float32 [3, 320, 320], P(None, 'clip')
All inputs are finite; a program needn't handle non-finite values.
Results may differ from a plain program's by a relative error of at most 0.0049.
Values may be sent and summed in bfloat16 or wider, within the bound.
A program may use at most 64 MiB of HBM per device.

v0:
```python
import math

import jax
import jax.numpy as jnp
from jax import lax
from jax.sharding import PartitionSpec as P


def padded_2(cells, sides, width):
    for axis, dim in sides:
        count = lax.axis_size(axis)
        ends = count - 1
        head = lax.slice_in_dim(cells, 0, width, axis=dim)
        tail = lax.slice_in_dim(cells, cells.shape[dim] - width, cells.shape[dim], axis=dim)
        cells = jnp.concatenate(
            [
                lax.ppermute(tail, axis, [(i, (i + 1) % count) for i in range(ends)]),
                cells,
                lax.ppermute(head, axis, [((i + 1) % count, i) for i in range(ends)]),
            ],
            axis=dim,
        )
    return cells


def outer_dot(left, right):
    return lax.dot_general(
        left, right, (((0,), (0,)), ((), ())), preferred_element_type=jnp.float32
    )


def transpose_dot(left, right):
    return lax.dot_general(
        left, right, (((1,), (1,)), ((), ())), preferred_element_type=jnp.float32
    )


def on_device(video, spatial_w, spatial_b, temporal_w, cotangent):
    clips, frames, height, width, chans = video.shape
    row_count = clips * frames * height * width
    video_b = video.astype(jnp.bfloat16)
    padded = jnp.pad(video_b, ((0, 0), (0, 0), (1, 1), (1, 1), (0, 0)))
    temporal_b = temporal_w.astype(jnp.bfloat16)
    spatial_all, temporal_all = (
        lax.all_gather(spatial_w, "clip", axis=1, tiled=True),
        lax.all_gather(temporal_b, "clip", axis=1, tiled=True),
    )
    spatial = jnp.zeros((row_count, chans), jnp.float32)
    for shift_y in range(3):
        for shift_x in range(3):
            window = padded[:, :, shift_y : shift_y + height, shift_x : shift_x + width, :].reshape(
                row_count, chans
            )
            spatial = spatial + jnp.dot(
                window, spatial_all[3 * shift_y + shift_x], preferred_element_type=jnp.float32
            )
    spatial = spatial + spatial_b
    sigmoid_s = jax.nn.sigmoid(spatial)
    hidden = (spatial * sigmoid_s).astype(jnp.bfloat16).reshape(clips, frames, height, width, chans)
    hidden_pad = padded_2(hidden, (("tm", 1),), 1)
    temporal = jnp.zeros((row_count, chans), jnp.float32)
    for kernel_tap in range(3):
        shifted = hidden_pad[:, kernel_tap : kernel_tap + frames].reshape(row_count, chans)
        temporal = temporal + jnp.dot(
            shifted, temporal_all[kernel_tap], preferred_element_type=jnp.float32
        )
    output = video + temporal.reshape(video.shape)
    cot_b = cotangent.astype(jnp.bfloat16)
    cot_flat = cot_b.reshape(row_count, chans)
    cot_pad = padded_2(cot_b, (("tm", 1),), 1)
    grad_hidden = jnp.zeros((row_count, chans), jnp.float32)
    grads = []
    for kernel_tap in range(3):
        shifted_cot = cot_pad[:, 2 - kernel_tap : 2 - kernel_tap + frames].reshape(row_count, chans)
        grad_hidden = grad_hidden + transpose_dot(shifted_cot, temporal_all[kernel_tap])
        shifted_hid = hidden_pad[:, kernel_tap : kernel_tap + frames].reshape(row_count, chans)
        grads.append(outer_dot(shifted_hid, cot_flat))
    local_grad = jnp.stack(grads)
    total_rows = row_count * lax.axis_size("tm") * lax.axis_size("clip")
    summed = lax.psum(local_grad, "tm")
    owned = lax.psum_scatter(summed, "clip", scatter_dimension=1, tiled=True)
    grad_temporal = owned * (1.0 / math.sqrt(total_rows))
    grad_spatial = (grad_hidden * sigmoid_s * (1.0 + spatial * (1.0 - sigmoid_s))).astype(
        jnp.bfloat16
    )
    grad_frames = jnp.pad(
        grad_spatial.reshape(clips, frames, height, width, chans),
        ((0, 0), (0, 0), (1, 1), (1, 1), (0, 0)),
    )
    grad_acc = cotangent.reshape(row_count, chans)
    for shift_y in range(3):
        for shift_x in range(3):
            window = grad_frames[
                :, :, 2 - shift_y : 2 - shift_y + height, 2 - shift_x : 2 - shift_x + width, :
            ].reshape(row_count, chans)
            grad_acc = grad_acc + transpose_dot(window, spatial_all[3 * shift_y + shift_x])
    grad_video = grad_acc.reshape(video.shape)
    return (output, grad_video, grad_temporal)


def solution(mesh):
    return jax.shard_map(
        on_device,
        mesh=mesh,
        in_specs=(
            P("clip", "tm", None, None, None),
            P(None, "clip", None),
            P(),
            P(None, "clip", None),
            P("clip", "tm", None, None, None),
        ),
        out_specs=(
            P("clip", "tm", None, None, None),
            P("clip", "tm", None, None, None),
            P(None, "clip", None),
        ),
        check_vma=False,
    )
```

profile of v0, /device:TPU:0, one launch (start us, length us, event | category | flops | bytes accessed | tf_op | source)
XLA Modules:
  0.0 184.8 jit_solution(11059689400053077663)
XLA Ops:
  7.2 0.0 all-gather.2.cloned.1.call-start
  7.2 0.7 all-gather.2.cloned.1.call-update
  7.9 0.0 reduce-scatter.2.cloned.1.call-start
  8.0 1.2 convert_element_type.21
  9.2 4.9 %collective-permute-start.3 = (bf16[1,1,16,32,320]{4,3,2,1,0:T(8,128)(2,1)S(1)}, bf16[1,1,16,32,320]{4,3,2,1,0:T(8,128)(2,1)S(1)}, u32[]{:S(2)}, u32[]{:S(2)}) collective-permute-start(bf16[1,1,16,32,320]{4,3,2,1,0:T(8,128)(2,1)S(1)} %convert_element_type.21), channel_id=1, source_target_pairs={{0,4},{4,8},{8,12},{12,16},{16,20},{20,24},{24,28},{1,5},{5,9},{9,... | collective-permute-start | bytes 983048 | tf_op jit(solution)/shard_map/ppermute | solution.py:17
  14.1 1.3 collective-permute-start.2
  15.5 10.1 %all_gather.7 = bf16[3,320,320]{2,1,0:T(8,128)(2,1)S(1)} all-gather(bf16[3,80,320]{2,1,0:T(8,128)(2,1)S(1)} %convert_element_type.20), channel_id=1, replica_groups=mesh['tm'=8,'clip'=4] {'clip'}, dimensions={1}, use_global_device_ids=true | all-gather | bytes 768000 | tf_op jit(solution)/shard_map/all_gather | solution.py:46
  25.6 1.8 pad_slice_fusion.8
  27.4 1.1 copy.16
  28.5 1.2 fusion.19
  29.7 1.1 collective-permute-done.3
  30.8 1.2 fusion.21
  32.0 4.5 %all-gather.2.cloned.1.call-done = bf16[9,320,320]{2,1,0:T(8,128)(2,1)} async-done(((bf16[9,80,320]{2,1,0:T(8,128)(2,1)}), bf16[9,320,320]{2,1,0:T(8,128)(2,1)}) %all-gather.2.cloned.1.call-update) | async-done | bytes 1843216 | tf_op jit(solution)/shard_map/all_gather | solution.py:45
  36.5 1.6 fusion.14
  38.1 1.5 convolution_add_fusion.14
  39.6 1.4 convolution_add_fusion.13
  41.0 0.4 convolution_add_fusion.12
  41.4 0.4 convolution_add_fusion.11
  41.8 0.2 copy-done.17
  42.0 0.4 convolution_add_fusion.10
  42.4 0.0 copy-done.16
  42.4 0.4 convolution_add_fusion.9
  42.8 0.1 copy-done.15
  42.9 0.4 convolution_add_fusion.8
  43.3 0.2 copy-done.20
  43.4 1.4 multiply_convert_fusion
  44.8 1.9 %copy.13 = bf16[512,320]{1,0:T(8,128)(2,1)} copy(bf16[512,320]{0,1:T(8,128)(2,1)} %get-tuple-element.22) | data formatting | bytes 655360 | tf_op jit(solution)/shard_map/convert_element_type | solution.py:59
  46.7 1.3 collective-permute-start.1
  48.0 5.9 %collective-permute-start = (bf16[1,1,16,32,320]{4,3,2,1,0:T(8,128)(2,1)}, bf16[1,1,16,32,320]{4,3,2,1,0:T(8,128)(2,1)}, u32[]{:S(2)}, u32[]{:S(2)}) collective-permute-start(bf16[1,1,16,32,320]{4,3,2,1,0:T(8,128)(2,1)} %bitcast.146), channel_id=1, source_target_pairs={{0,4},{4,8},{8,12},{12,16},{16,20},{20,24},{24,28},{1,5},{5,9},{9,... | collective-permute-start | bytes 983048 | tf_op jit(solution)/shard_map/ppermute | solution.py:17
  53.9 2.8 %fusion.9 = bf16[512,320]{0,1:T(8,128)(2,1)} fusion(f32[512,320]{0,1:T(8,128)} %fusion.21, f32[512,320]{0,1:T(8,128)} %fusion.19, bf16[512,320]{1,0:T(8,128)(2,1)} %bitcast.26, f32[512,320]{0,1:T(8,128)} %get-tuple-element.23, bf16[3,320,320]{2,1,0:T(8,128)(2,1)S(1)} %all_gather.7), kind=kOutput, calls=%fused_computation.25 | convolution fusion | flops 106659840 | bytes 2867200 | tf_op jit(solution)/shard_map/dot_general | solution.py:33
  56.7 1.9 %copy.15 = bf16[512,320]{1,0:T(8,128)(2,1)} copy(bf16[512,320]{0,1:T(8,128)(2,1)} %fusion.9) | data formatting | bytes 655360 | tf_op jit(solution)/shard_map/convert_element_type | solution.py:83
  58.6 4.4 %pad_slice_fusion.4 = (bf16[1,1,16,32,320]{4,3,2,1,0:T(8,128)(2,1)}, bf16[1,1,16,32,320]{4,3,2,1,0:T(8,128)(2,1)}, bf16[1,1,16,32,320]{4,3,2,1,0:T(8,128)(2,1)},...) fusion(bf16[1,1,16,32,320]{4,3,2,1,0:T(8,128)(2,1)} %bitcast.132), kind=kLoop, calls=%fused_computation.35 | loop fusion | bytes 2949120 | tf_op jit(solution)/shard_map/slice | solution.py:93
  63.0 1.2 fusion.15
  64.3 0.3 convolution_bitcast_fusion.1
  64.6 1.4 convolution_bitcast_fusion
  66.0 3.7 %collective-permute-done = bf16[1,1,16,32,320]{4,3,2,1,0:T(8,128)(2,1)} collective-permute-done((bf16[1,1,16,32,320]{4,3,2,1,0:T(8,128)(2,1)}, bf16[1,1,16,32,320]{4,3,2,1,0:T(8,128)(2,1)}, u32[]{:S(2)}, u32[]{:S(2)}) %collective-permute-start) | collective-permute-done | bytes 327712 | tf_op jit(solution)/shard_map/ppermute | solution.py:17
  69.6 1.3 convolution_bitcast_fusion.2
  71.0 1.2 pad_maximum_fusion
  72.3 0.0 reduce-scatter.2.cloned.1.call-update
  72.3 0.0 all-reduce.4.cloned.1.call-start
  72.3 1.4 fusion.16
  73.8 1.4 fusion.17
  75.2 0.4 fusion.18
  75.6 0.4 convolution_add_fusion.4
  76.0 0.0 copy-start.11
  76.0 0.4 convolution_add_fusion.3
  76.4 0.2 copy-done.12
  76.6 0.4 convolution_add_fusion.2
  77.0 0.1 copy-done.11
  77.0 0.4 convolution_add_fusion.1
  77.4 0.1 copy-done.8
  77.5 0.1 copy-done.19
  77.6 1.2 fusion.3
  78.9 2.3 %copy.17 = f32[512,320]{1,0:T(8,128)} copy(f32[512,320]{0,1:T(8,128)} %fusion.3) | data formatting | bytes 1310720 | tf_op jit(solution)/shard_map/add | solution.py:96
  81.1 0.4 fusion.20
  81.5 20.0 %reduce-scatter.2.cloned.1.call-done = f32[3,80,320]{2,1,0:T(8,128)} async-done(((f32[3,320,320]{2,1,0:T(8,128)}), f32[3,80,320]{2,1,0:T(8,128)}) %reduce-scatter.2.cloned.1.call-update) | async-done | bytes 307216 | tf_op jit(solution)/shard_map/reduce_scatter | solution.py:81
  101.5 0.0 all-reduce.4.cloned.1.call-update
  101.6 1.4 fusion.22
  102.9 0.0 copy-start.5
  103.0 2.3 %fusion.7 = f32[512,320]{0,1:T(8,128)} fusion(f32[512,320]{0,1:T(8,128)S(1)} %fusion.22, f32[512,320]{0,1:T(8,128)S(1)} %fusion.20, bf16[512,320]{1,0:T(8,128)(2,1)} %bitcast.19, bf16[3,320,320]{2,1,0:T(8,128)(2,1)S(1)} %all_gather.7), kind=kOutput, calls=%fused_computation.15 | convolution fusion | flops 105185280 | bytes 2539520 | tf_op jit(solution)/shard_map/dot_general | solution.py:64
  105.2 1.3 copy.14
  106.6 1.0 add.101
  107.6 69.0 %all-reduce.4.cloned.1.call-done = f32[3,80,320]{2,1,0:T(8,128)} async-done(((f32[3,80,320]{2,1,0:T(8,128)}), f32[3,80,320]{2,1,0:T(8,128)}) %all-reduce.4.cloned.1.call-update) | async-done | bytes 307216 | tf_op jit(solution)/shard_map/psum | solution.py:80
  176.5 1.7 broadcast_multiply_fusion
  (40 shorter events, 0.2 us)
Async XLA Ops:
  7.2 8.2 %copy-start.4 = (f32[1,1,16,32,320]{4,3,2,1,0:T(8,128)S(1)}, f32[1,1,16,32,320]{4,3,2,1,0:T(8,128)}, u32[]{:S(2)}) copy-start(f32[1,1,16,32,320]{4,3,2,1,0:T(8,128)} %param.5) | copy-start | bytes 1966084
  7.2 8.2 %copy-start.21 = (f32[3,80,320]{2,1,0:T(8,128)S(1)}, f32[3,80,320]{2,1,0:T(8,128)}, u32[]{:S(2)}) copy-start(f32[3,80,320]{2,1,0:T(8,128)} %param.8) | copy-start | bytes 921604
  7.2 29.3 %all-gather.2.cloned.1.call-start = ((), (), s32[]{:S(2)}) async-start(), calls=%async_computation.1 | async-start | bytes 2764800 | tf_op jit(solution)/shard_map/all_gather | solution.py:45
  7.9 93.6 %reduce-scatter.2.cloned.1.call-start = ((), (), s32[]{:S(2)}) async-start(), calls=%async_computation.2 | async-start | bytes 1843200 | tf_op jit(solution)/shard_map/reduce_scatter | solution.py:81
  9.2 21.7 %collective-permute-start.3 = (bf16[1,1,16,32,320]{4,3,2,1,0:T(8,128)(2,1)S(1)}, bf16[1,1,16,32,320]{4,3,2,1,0:T(8,128)(2,1)S(1)}, u32[]{:S(2)}, u32[]{:S(2)}) collective-permute-start(bf16[1,1,16,32,320]{4,3,2,1,0:T(8,128)(2,1)S(1)} %convert_element_type.21), channel_id=1, source_target_pairs={{0,4},{4,8},{8,12},{12,16},{16,20},{20,24},{24,28},{1,5},{5,9},{9,... | collective-permute-start | bytes 983048 | tf_op jit(solution)/shard_map/ppermute | solution.py:17
  14.1 39.9 %collective-permute-start.2 = (bf16[1,1,16,32,320]{4,3,2,1,0:T(8,128)(2,1)S(1)}, bf16[1,1,16,32,320]{4,3,2,1,0:T(8,128)(2,1)}, u32[]{:S(2)}, u32[]{:S(2)}) collective-permute-start(bf16[1,1,16,32,320]{4,3,2,1,0:T(8,128)(2,1)S(1)} %convert_element_type.21), channel_id=1, source_target_pairs={{4,0},{8,4},{12,8},{16,12},{20,16},{24,20},{28,24},{5,1},{9,5},{13... | collective-permute-start | bytes 983048 | tf_op jit(solution)/shard_map/ppermute | solution.py:19
  15.4 11.9 %copy-start.1 = (bf16[1,1,16,32,320]{4,3,2,1,0:T(8,128)(2,1)}, bf16[1,1,16,32,320]{4,3,2,1,0:T(8,128)(2,1)S(1)}, u32[]{:S(2)}) copy-start(bf16[1,1,16,32,320]{4,3,2,1,0:T(8,128)(2,1)S(1)} %convert_element_type.18) | copy-start | bytes 983044
  15.5 11.9 %copy-start.3 = (f32[1,1,16,32,320]{4,3,2,1,0:T(8,128)S(1)}, f32[1,1,16,32,320]{4,3,2,1,0:T(8,128)}, u32[]{:S(2)}) copy-start(f32[1,1,16,32,320]{4,3,2,1,0:T(8,128)} %param.9) | copy-start | bytes 1966084
  36.5 3.1 %copy-start = (bf16[9,320,320]{2,1,0:T(8,128)(2,1)S(1)}, bf16[9,320,320]{2,1,0:T(8,128)(2,1)}, u32[]{:S(2)}) copy-start(bf16[9,320,320]{2,1,0:T(8,128)(2,1)} %all-gather.2.cloned.1.call-done) | copy-start | bytes 5529604
  38.1 3.0 %copy-start.18 = (bf16[1,1,16,32,320]{4,3,2,1,0:T(8,128)(2,1)S(1)}, bf16[1,1,16,32,320]{4,3,2,1,0:T(8,128)(2,1)}, u32[]{:S(2)}) copy-start(bf16[1,1,16,32,320]{4,3,2,1,0:T(8,128)(2,1)} %get-tuple-element.17) | copy-start | bytes 983044
  39.6 1.9 %copy-start.2 = (bf16[1,1,16,32,320]{4,3,2,1,0:T(8,128)(2,1)S(1)}, bf16[1,1,16,32,320]{4,3,2,1,0:T(8,128)(2,1)}, u32[]{:S(2)}) copy-start(bf16[1,1,16,32,320]{4,3,2,1,0:T(8,128)(2,1)} %copy-done.1) | copy-start | bytes 983044
  41.0 1.0 copy-start.17
  41.4 1.0 copy-start.16
  41.8 1.1 copy-start.15
  42.4 1.0 copy-start.20
  42.4 1.0 copy-start.22
  46.7 17.9 %collective-permute-start.1 = (bf16[1,1,16,32,320]{4,3,2,1,0:T(8,128)(2,1)}, bf16[1,1,16,32,320]{4,3,2,1,0:T(8,128)(2,1)}, u32[]{:S(2)}, u32[]{:S(2)}) collective-permute-start(bf16[1,1,16,32,320]{4,3,2,1,0:T(8,128)(2,1)} %bitcast.145), channel_id=1, source_target_pairs={{4,0},{8,4},{12,8},{16,12},{20,16},{24,20},{28,24},{5,1},{9,5},{13... | collective-permute-start | bytes 983048 | tf_op jit(solution)/shard_map/ppermute | solution.py:19
  48.0 21.6 %collective-permute-start = (bf16[1,1,16,32,320]{4,3,2,1,0:T(8,128)(2,1)}, bf16[1,1,16,32,320]{4,3,2,1,0:T(8,128)(2,1)}, u32[]{:S(2)}, u32[]{:S(2)}) collective-permute-start(bf16[1,1,16,32,320]{4,3,2,1,0:T(8,128)(2,1)} %bitcast.146), channel_id=1, source_target_pairs={{0,4},{4,8},{8,12},{12,16},{16,20},{20,24},{24,28},{1,5},{5,9},{9,... | collective-permute-start | bytes 983048 | tf_op jit(solution)/shard_map/ppermute | solution.py:17
  58.6 5.6 %copy-start.6 = (bf16[512,320]{0,1:T(8,128)(2,1)S(1)}, bf16[512,320]{0,1:T(8,128)(2,1)}, u32[]{:S(2)}) copy-start(bf16[512,320]{0,1:T(8,128)(2,1)} %get-tuple-element.22) | copy-start | bytes 983044
  72.2 3.0 %copy-start.10 = (bf16[1,1,16,32,320]{4,3,2,1,0:T(8,128)(2,1)S(1)}, bf16[1,1,16,32,320]{4,3,2,1,0:T(8,128)(2,1)}, u32[]{:S(2)}) copy-start(bf16[1,1,16,32,320]{4,3,2,1,0:T(8,128)(2,1)} %get-tuple-element.12) | copy-start | bytes 983044
  72.3 104.3 %all-reduce.4.cloned.1.call-start = ((), (), s32[]{:S(2)}) async-start(), calls=%async_computation.3 | async-start | bytes 737280 | tf_op jit(solution)/shard_map/psum | solution.py:80
  72.3 3.3 %copy-start.9 = (f32[512,320]{0,1:T(8,128)S(1)}, f32[512,320]{0,1:T(8,128)}, u32[]{:S(2)}) copy-start(f32[512,320]{0,1:T(8,128)} %copy.16) | copy-start | bytes 1966084
  72.3 3.3 %copy-start.14 = (bf16[1,1,16,32,320]{4,3,2,1,0:T(8,128)(2,1)S(1)}, bf16[1,1,16,32,320]{4,3,2,1,0:T(8,128)(2,1)}, u32[]{:S(2)}) copy-start(bf16[1,1,16,32,320]{4,3,2,1,0:T(8,128)(2,1)} %get-tuple-element.13) | copy-start | bytes 983044
  73.8 2.2 %copy-start.13 = (bf16[1,1,16,32,320]{4,3,2,1,0:T(8,128)(2,1)S(1)}, bf16[1,1,16,32,320]{4,3,2,1,0:T(8,128)(2,1)}, u32[]{:S(2)}) copy-start(bf16[1,1,16,32,320]{4,3,2,1,0:T(8,128)(2,1)} %get-tuple-element.7) | copy-start | bytes 983044
  75.6 1.0 copy-start.12
  76.0 1.0 copy-start.11
  76.4 1.1 copy-start.8
  76.4 1.2 copy-start.19
  77.6 3.5 %copy-start.7 = (bf16[512,320]{0,1:T(8,128)(2,1)S(1)}, bf16[512,320]{0,1:T(8,128)(2,1)}, u32[]{:S(2)}) copy-start(bf16[512,320]{0,1:T(8,128)(2,1)} %get-tuple-element.22) | copy-start | bytes 983044
  102.9 3.7 %copy-start.5 = (f32[1,1,16,32,320]{4,3,2,1,0:T(8,128)S(1)}, f32[1,1,16,32,320]{4,3,2,1,0:T(8,128)}, u32[]{:S(2)}) copy-start(f32[1,1,16,32,320]{4,3,2,1,0:T(8,128)} %param.5) | copy-start | bytes 1966084
Sparse Core Ops, SparseCore 0:
  9.6 26.8 all-gather.1
  72.4 29.1 reduce-scatter.1
  104.9 71.5 all-reduce.3
where the time goes:
time: 186 us; the launch traced here: 185 us
  waiting for transfers between devices  99 us (53%)
  matrix products  27.1 us (15%)
  local copies, waits for them, and re-layouts  15.7 us (8%)
  between operations  14.2 us (8%)
  starting transfers between devices  13.5 us (7%)
  blocking collectives  10.1 us (5%)
  other arithmetic  5.23 us (3%)
    psum x1, waiting for transfers between devices, on_device(): summed = lax.psum(local_grad, 'tm')  69 us
    reduce_scatter x1, waiting for transfers between devices, on_device(): owned = lax.psum_scatter(summed, 'clip', scatter_dimension=1, tiled=True)  20 us
    dot_general x12, matrix products, transpose_dot(): lax.dot_general(left, right, (((1,), (1,)), ((), ())), preferred_element_...  12.3 us
    ppermute x2, starting transfers between devices, padded_2(): lax.ppermute(tail, axis, [(i, (i + 1) % count) for i in range(ends)])  10.8 us
    all_gather x1, blocking collectives, on_device(): lax.all_gather(temporal_b, 'clip', axis=1, tiled=True)  10.1 us
    dot_general x9, matrix products, on_device(): jnp.dot(window, spatial_all[3 * shift_y + shift_x], preferred_element_typ...  7.74 us
    ppermute x2, waiting for transfers between devices, padded_2(): lax.ppermute(tail, axis, [(i, (i + 1) % count) for i in range(ends)])  4.81 us
    all_gather x1, waiting for transfers between devices, on_device(): lax.all_gather(spatial_w, 'clip', axis=1, tiled=True)  4.46 us
  transfers between devices with their start and end apart: 7, of which 5 were waited for; matrix products, arithmetic and copies ran while one was open for 23% of the time, Pallas kernels for 0%

commit v1 on v0

v1 whole, which is shorter than its diff:
```python
import functools
import math

import jax
import jax.numpy as jnp
from jax import lax
from jax.experimental import pallas as pl
from jax.experimental.pallas import tpu as pltpu
from jax.sharding import PartitionSpec as P

F32 = jnp.float32
BF16 = jnp.bfloat16
MESH = pl.DeviceIdType.MESH


def nn_dot(left, right):
    return lax.dot_general(left, right, (((1,), (0,)), ((), ())), preferred_element_type=F32)


def outer_dot(left, right):
    return lax.dot_general(left, right, (((0,), (0,)), ((), ())), preferred_element_type=F32)


def transpose_dot(left, right):
    return lax.dot_general(left, right, (((1,), (1,)), ((), ())), preferred_element_type=F32)


def block_kernel(
    dims,
    video_h, sw_h, bias_ref, tw_h, cot_h,
    out_h, gv_h, gt_h,
    video, cot, tw, wg, xcat, cb, chalo, hb, hhalo, slope, gpad, out_v, gv_v,
    gtl, rx, ysend, ry, psum, pb, rs, mine, ag, gt_v,
    load_sem, w_send, w_recv, halo_send, halo_recv, g_send, g_recv, a_send, a_recv, out_sem,
):
    n_tm, height, width, chans, scale = dims
    rows = height * width
    depth = sw_h.shape[1]
    half = rows // 2
    tm = lax.axis_index("tm")
    c = lax.axis_index("clip")

    def flip(value, bit):
        return value + bit - 2 * bit * (lax.rem(value // bit, 2))

    core, ypart = flip(c, 1), flip(c, 2)
    xpart, zpart = flip(tm, 1), flip(tm, 2)
    parity = lax.rem(tm, 2)
    h = lax.rem(tm // 2, 2)

    loads = [
        pltpu.make_async_copy(cot_h, cot, load_sem.at[0]),
        pltpu.make_async_copy(tw_h, tw, load_sem.at[1]),
        pltpu.make_async_copy(
            sw_h, wg.at[pl.ds(0, 9), pl.ds(pl.multiple_of(c * depth, 16), depth), :], load_sem.at[2]
        ),
        pltpu.make_async_copy(video_h, video, load_sem.at[3]),
    ]
    for load in loads:
        load.start()

    barrier = pltpu.get_barrier_semaphore()
    for step in range(1, n_tm):
        pl.semaphore_signal(
            barrier, inc=1, device_id=(lax.rem(tm + step, n_tm), c), device_id_type=MESH
        )
    pl.semaphore_signal(barrier, inc=1, device_id=(tm, core), device_id_type=MESH)
    pl.semaphore_signal(barrier, inc=1, device_id=(tm, ypart), device_id_type=MESH)

    def band(owner, first, count=3):
        return wg.at[pl.ds(first, count), pl.ds(pl.multiple_of(owner * depth, 16), depth), :]

    loads[0].wait()
    cb[...] = cot[...].astype(BF16)
    loads[1].wait()
    wg[9:12, pl.ds(pl.multiple_of(c * depth, 16), depth), :] = tw[...].astype(BF16)
    loads[2].wait()
    pl.semaphore_wait(barrier, n_tm + 1)

    def send(src, dst, ssem, rsem, device):
        copy = pltpu.make_async_remote_copy(
            src_ref=src, dst_ref=dst, send_sem=ssem, recv_sem=rsem,
            device_id=device, device_id_type=MESH,
        )
        copy.start()
        return copy

    def wsend(slot, owner, first, device):
        return send(band(owner, first), band(owner, first), w_send.at[slot], w_recv.at[slot], device)

    y_copies = [wsend(j, c, 6 * h + 3 * j, (tm, ypart)) for j in range(2)]

    def hsend(slot, src, dst, device):
        return send(src, dst, halo_send.at[slot], halo_recv.at[slot], device)

    def near_sends(base, own, halo):
        return [
            hsend(
                base + q,
                own.at[pl.ds(q * half, half), :],
                halo.at[parity, pl.ds(q * half, half), :],
                (xpart, c),
            )
            for q in range(2)
        ]

    def far_copy(base, halo, q):
        target = tm + 2 - 4 * parity
        target = jnp.clip(target, 0, n_tm - 1)
        return pltpu.make_async_remote_copy(
            src_ref=halo.at[1 - parity, pl.ds(q * half, half), :],
            dst_ref=halo.at[parity, pl.ds(q * half, half), :],
            send_sem=halo_send.at[base + 2 + q],
            recv_sem=halo_recv.at[base + 2 + q],
            device_id=(target, c),
            device_id_type=MESH,
        )

    sends_far = jnp.logical_or(
        jnp.logical_and(parity == 0, tm + 2 < n_tm), jnp.logical_and(parity == 1, tm >= 2)
    )
    gets_far = jnp.logical_or(
        jnp.logical_and(parity == 0, tm >= 2), jnp.logical_and(parity == 1, tm + 2 < n_tm)
    )

    def far_start(base, halo, q):
        @pl.when(sends_far)
        def _():
            far_copy(base, halo, q).start()

    def far_recv(base, halo, q):
        @pl.when(gets_far)
        def _():
            far_copy(base, halo, q).wait_recv()

    def far_done(base, halo, q):
        @pl.when(sends_far)
        def _():
            far_copy(base, halo, q).wait_send()

    cot_near = near_sends(0, cb, chalo)
    own_copies = [wsend(4 + j, c, 3 * j, (tm, core)) for j in range(4)]

    for edge, slot in ((0, 0), (n_tm - 1, 1)):
        @pl.when(tm == edge)
        def _():
            chalo[slot] = jnp.zeros((rows, chans), BF16)
            hhalo[slot] = jnp.zeros((rows, chans), BF16)

    column = lax.rem(lax.broadcasted_iota(jnp.int32, (rows, chans), 0), width)

    def shifted(value, step):
        if step == 0:
            return value
        rolled = pltpu.roll(value, step % rows, 0)
        return jnp.where(column == (0 if step == 1 else width - 1), 0.0, rolled)

    xcat[0:width] = jnp.zeros((width, 3 * chans), BF16)
    xcat[width + rows :] = jnp.zeros((width, 3 * chans), BF16)
    for b in range(3):
        gpad[b, 0:width] = jnp.zeros((width, chans), BF16)
        gpad[b, width + rows :] = jnp.zeros((width, chans), BF16)
    loads[3].wait()
    frame = video[...]
    xcat[width : width + rows] = jnp.concatenate(
        [shifted(frame, 1).astype(BF16), frame.astype(BF16), shifted(frame, -1).astype(BF16)], axis=1
    )

    relays = []
    z_copies = []
    for j in range(2):
        y_copies[j].wait_recv()
        z_copies.append(wsend(2 + j, ypart, 6 * h + 3 * j, (zpart, c)))
        relays.append(wsend(8 + j, ypart, 6 * h + 3 * j, (tm, core)))
        cot_near[j].wait_recv()
        far_start(0, chalo, j)
    for j in range(2):
        z_copies[j].wait_recv()
        relays.append(wsend(10 + j, ypart, 6 * (1 - h) + 3 * j, (tm, core)))
    for copy in own_copies + relays:
        copy.wait_recv()

    hid_near = []
    for q in range(2):
        acc = bias_ref[...] + jnp.zeros((half, chans), F32)
        for a in range(3):
            acc = acc + nn_dot(
                xcat[a * width + q * half : a * width + (q + 1) * half],
                wg[3 * a : 3 * a + 3].reshape(3 * chans, chans),
            )
        sig = jax.nn.sigmoid(acc)
        hb[q * half : (q + 1) * half] = (acc * sig).astype(BF16)
        slope[q * half : (q + 1) * half] = sig * (1.0 + acc * (1.0 - sig))
        hid_near.append(
            hsend(
                4 + q,
                hb.at[pl.ds(q * half, half), :],
                hhalo.at[parity, pl.ds(q * half, half), :],
                (xpart, c),
            )
        )

    for q in range(2):
        far_recv(0, chalo, q)
    n_own = chans // depth
    pad_rows = psum.shape[0]
    hidden_all = hb[...]
    for k in range(3):
        right = (chalo[1], cb[...], chalo[0])[k]
        product = outer_dot(hidden_all, right)
        for owner in range(n_own):
            gtl[owner, k * depth : (k + 1) * depth] = product[owner * depth : (owner + 1) * depth]
    for owner in range(n_own):
        gtl[owner, 3 * depth :] = jnp.zeros((pad_rows - 3 * depth, chans), F32)
    diag = flip(core, 2)
    core_copies = [
        send(gtl.at[diag], rx.at[1], g_send.at[0], g_recv.at[0], (tm, core)),
        send(gtl.at[core], rx.at[0], g_send.at[1], g_recv.at[1], (tm, core)),
    ]

    grad_h = transpose_dot(chalo[1], wg[9]) + transpose_dot(cb[...], wg[10])
    grad_h = grad_h + transpose_dot(chalo[0], wg[11])
    grad_s = grad_h * slope[...]
    for b in range(3):
        gpad[b, width : width + rows] = shifted(grad_s, b - 1).astype(BF16)

    core_copies[0].wait_recv()
    ysend[...] = (gtl[ypart] + rx[1]).astype(BF16)
    grad_y = send(ysend, ry, g_send.at[2], g_recv.at[2], (tm, ypart))
    core_copies[1].wait_recv()
    psum[...] = gtl[c] + rx[0]

    hid_near[0].wait_recv()
    far_start(4, hhalo, 0)

    def grad_conv(q):
        acc = cot[q * half : (q + 1) * half]
        for a in range(3):
            start = (2 - a) * width + q * half
            for b in range(3):
                acc = acc + transpose_dot(gpad[b, start : start + half], wg[3 * a + b])
        gv_v[q * half : (q + 1) * half] = acc

    grad_conv(0)
    hid_near[1].wait_recv()
    far_start(4, hhalo, 1)

    grad_y.wait_recv()
    psum[...] = psum[...] + ry[...].astype(F32)
    pb[...] = psum[...].astype(BF16)
    piece = pad_rows // n_tm
    scatters = []
    for step in range(1, n_tm):
        to = lax.rem(tm + step, n_tm)
        scatters.append(
            send(
                pb.at[pl.ds(pl.multiple_of(to * piece, piece), piece), :],
                rs.at[step - 1], a_send.at[step - 1], a_recv.at[step - 1], (to, c),
            )
        )
    grad_conv(1)
    gv_out = pltpu.make_async_copy(gv_v, gv_h, out_sem.at[0])
    gv_out.start()

    out_v[...] = video[...] + nn_dot(hb[...], wg[10])

    for copy in scatters:
        copy.wait_recv()
    total = psum[pl.ds(pl.multiple_of(tm * piece, piece), piece), :]
    for step in range(1, n_tm):
        total = total + rs[step - 1].astype(F32)
    spot = pl.ds(pl.multiple_of(tm * piece, piece), piece)
    mine[...] = total.astype(BF16)
    gathers = []
    for step in range(1, n_tm):
        to = lax.rem(tm + step, n_tm)
        slot = n_tm - 2 + step
        gathers.append(
            send(mine, ag.at[spot, :], a_send.at[slot], a_recv.at[slot], (to, c))
        )
    ag[spot, :] = total.astype(BF16)

    for q in range(2):
        far_recv(4, hhalo, q)
    out_v[...] = out_v[...] + nn_dot(hhalo[0], wg[9]) + nn_dot(hhalo[1], wg[11])
    out_out = pltpu.make_async_copy(out_v, out_h, out_sem.at[1])
    out_out.start()

    for copy in gathers:
        copy.wait_recv()
    gt_v[...] = (ag[0 : 3 * depth].astype(F32) * scale).reshape(3, depth, chans)
    gt_out = pltpu.make_async_copy(gt_v, gt_h, out_sem.at[2])
    gt_out.start()

    for copy in (
        y_copies + z_copies + own_copies + relays + cot_near + hid_near
        + core_copies + [grad_y] + scatters + gathers
    ):
        copy.wait_send()
    for q in range(2):
        far_done(0, chalo, q)
        far_done(4, hhalo, q)
    gv_out.wait()
    out_out.wait()
    gt_out.wait()


def fused(n_tm, n_clip, video, spatial_w, spatial_b, temporal_w, cotangent):
    clips, frames, height, width, chans = video.shape
    rows = height * width
    depth = spatial_w.shape[1]
    pad_rows = -(-3 * depth // (16 * n_tm)) * 16 * n_tm
    scale = 1.0 / math.sqrt(rows * n_tm * n_clip)
    piece = pad_rows // n_tm
    any_spec = pl.BlockSpec(memory_space=pl.ANY)
    vm = pltpu.VMEM
    dma = pltpu.SemaphoreType.DMA
    out, gv, gt = pl.pallas_call(
        functools.partial(block_kernel, (n_tm, height, width, chans, scale)),
        out_shape=(
            jax.ShapeDtypeStruct((rows, chans), F32),
            jax.ShapeDtypeStruct((rows, chans), F32),
            jax.ShapeDtypeStruct((3, depth, chans), F32),
        ),
        in_specs=[any_spec, any_spec, pl.BlockSpec(memory_space=vm), any_spec, any_spec],
        out_specs=(any_spec, any_spec, any_spec),
        scratch_shapes=[
            vm((rows, chans), F32),
            vm((rows, chans), F32),
            vm((3, depth, chans), F32),
            vm((12, chans, chans), BF16),
            vm((rows + 2 * width, 3 * chans), BF16),
            vm((rows, chans), BF16),
            vm((2, rows, chans), BF16),
            vm((rows, chans), BF16),
            vm((2, rows, chans), BF16),
            vm((rows, chans), F32),
            vm((3, rows + 2 * width, chans), BF16),
            vm((rows, chans), F32),
            vm((rows, chans), F32),
            vm((n_clip, pad_rows, chans), F32),
            vm((2, pad_rows, chans), F32),
            vm((pad_rows, chans), BF16),
            vm((pad_rows, chans), BF16),
            vm((pad_rows, chans), F32),
            vm((pad_rows, chans), BF16),
            vm((n_tm - 1, piece, chans), BF16),
            vm((piece, chans), BF16),
            vm((pad_rows, chans), BF16),
            vm((3, depth, chans), F32),
            dma((4,)),
            dma((12,)),
            dma((12,)),
            dma((8,)),
            dma((8,)),
            dma((3,)),
            dma((3,)),
            dma((2 * n_tm - 2,)),
            dma((2 * n_tm - 2,)),
            dma((3,)),
        ],
        compiler_params=pltpu.CompilerParams(
            collective_id=0, has_side_effects=True, vmem_limit_bytes=48 * 2**20
        ),
        name="block",
    )(
        video.reshape(rows, chans), spatial_w, spatial_b.reshape(1, chans), temporal_w,
        cotangent.reshape(rows, chans),
    )
    return out.reshape(video.shape), gv.reshape(video.shape), gt


def padded_2(cells, sides, width):
    for axis, dim in sides:
        count = lax.axis_size(axis)
        ends = count - 1
        head = lax.slice_in_dim(cells, 0, width, axis=dim)
        tail = lax.slice_in_dim(cells, cells.shape[dim] - width, cells.shape[dim], axis=dim)
        cells = jnp.concatenate(
            [
                lax.ppermute(tail, axis, [(i, (i + 1) % count) for i in range(ends)]),
                cells,
                lax.ppermute(head, axis, [((i + 1) % count, i) for i in range(ends)]),
            ],
            axis=dim,
        )
    return cells


def native(video, spatial_w, spatial_b, temporal_w, cotangent):
    clips, frames, height, width, chans = video.shape
    row_count = clips * frames * height * width
    pads = ((0, 0), (0, 0), (1, 1), (1, 1), (0, 0))
    padded = jnp.pad(video.astype(BF16), pads)
    temporal_b = temporal_w.astype(BF16)
    spatial_all = lax.all_gather(spatial_w, "clip", axis=1, tiled=True)
    temporal_all = lax.all_gather(temporal_b, "clip", axis=1, tiled=True)
    spatial = jnp.zeros((row_count, chans), F32)
    for y in range(3):
        for x in range(3):
            window = padded[:, :, y : y + height, x : x + width, :].reshape(row_count, chans)
            spatial = spatial + nn_dot(window, spatial_all[3 * y + x])
    spatial = spatial + spatial_b
    sigmoid_s = jax.nn.sigmoid(spatial)
    hidden = (spatial * sigmoid_s).astype(BF16).reshape(video.shape)
    hidden_pad = padded_2(hidden, (("tm", 1),), 1)
    cot_b = cotangent.astype(BF16)
    cot_flat = cot_b.reshape(row_count, chans)
    cot_pad = padded_2(cot_b, (("tm", 1),), 1)
    temporal = jnp.zeros((row_count, chans), F32)
    grad_hidden = jnp.zeros((row_count, chans), F32)
    grads = []
    for k in range(3):
        shifted_hid = hidden_pad[:, k : k + frames].reshape(row_count, chans)
        temporal = temporal + nn_dot(shifted_hid, temporal_all[k])
        shifted_cot = cot_pad[:, 2 - k : 2 - k + frames].reshape(row_count, chans)
        grad_hidden = grad_hidden + transpose_dot(shifted_cot, temporal_all[k])
        grads.append(outer_dot(shifted_hid, cot_flat))
    total_rows = row_count * lax.axis_size("tm") * lax.axis_size("clip")
    summed = lax.psum(jnp.stack(grads), "tm")
    owned = lax.psum_scatter(summed, "clip", scatter_dimension=1, tiled=True)
    grad_spatial = (grad_hidden * sigmoid_s * (1.0 + spatial * (1.0 - sigmoid_s))).astype(BF16)
    grad_frames = jnp.pad(grad_spatial.reshape(video.shape), pads)
    grad_acc = cotangent.reshape(row_count, chans)
    for y in range(3):
        for x in range(3):
            window = grad_frames[:, :, 2 - y : 2 - y + height, 2 - x : 2 - x + width, :]
            window = window.reshape(row_count, chans)
            grad_acc = grad_acc + transpose_dot(window, spatial_all[3 * y + x])
    return (
        video + temporal.reshape(video.shape),
        grad_acc.reshape(video.shape),
        owned * (1.0 / math.sqrt(total_rows)),
    )


def solution(mesh):
    n_tm, n_clip = mesh.shape["tm"], mesh.shape["clip"]

    def on_device(video, spatial_w, spatial_b, temporal_w, cotangent):
        args = (video, spatial_w, spatial_b, temporal_w, cotangent)
        one_frame = video.shape[0] == 1 and video.shape[1] == 1
        if one_frame and spatial_w.shape[1] % 16 == 0 and n_clip == 4 and n_tm % 4 == 0:
            return fused(n_tm, n_clip, *args)
        return native(*args)

    return jax.shard_map(
        on_device,
        mesh=mesh,
        in_specs=(
            P("clip", "tm", None, None, None),
            P(None, "clip", None),
            P(),
            P(None, "clip", None),
            P("clip", "tm", None, None, None),
        ),
        out_specs=(
            P("clip", "tm", None, None, None),
            P("clip", "tm", None, None, None),
            P(None, "clip", None),
        ),
        check_vma=False,
    )
```

time: 186 us -> 63 us (0.34)
  waiting for transfers between devices: 99 us -> 0 us
  Pallas kernels: 0 us -> 54.5 us
  matrix products: 27.1 us -> 0 us
  between operations: 14.2 us -> 0.65 us
  starting transfers between devices: 13.5 us -> 0 us
  blocking collectives: 10.1 us -> 0 us
  local copies, waits for them, and re-layouts: 15.7 us -> 7.48 us
  other arithmetic: 5.23 us -> 0 us
    psum x1 -> x0, waiting for transfers between devices: 69 us -> none  [on_device(): summed = lax.psum(local_grad, 'tm')]
    pallas_call x0 -> x1, Pallas kernels: none -> 54.5 us  [fused(): pl.pallas_call(functools.partial(block_kernel, (n_tm, height, width, chan...]
    dot_general x27 -> x0, matrix products: 27.1 us -> none  [the longest x12 12.3 us: transpose_dot(): lax.dot_general(left, right, (((1,), (1,)), ((), ())), preferred_element_...]
    reduce_scatter x1 -> x0, waiting for transfers between devices: 20 us -> none  [on_device(): owned = lax.psum_scatter(summed, 'clip', scatter_dimension=1, tiled=True)]
    ppermute x4 -> x0, starting transfers between devices: 13.4 us -> none  [the longest x2 10.8 us: padded_2(): lax.ppermute(tail, axis, [(i, (i + 1) % count) for i in range(ends)])]
    all_gather x1 -> x0, blocking collectives: 10.1 us -> none  [on_device(): lax.all_gather(temporal_b, 'clip', axis=1, tiled=True)]
    unnamed x46 -> x13, local copies, waits for them, and re-layouts: 0.99 us -> 7.48 us
    slice x2 -> x0, local copies, waits for them, and re-layouts: 6.2 us -> none  [the longest x1 4.41 us: on_device(): grad_frames[:, :, 2 - shift_y:2 - shift_y + height, 2 - shift_x:2 - shift...]
  transfers between devices with their start and end apart: 7 -> 0, of which waited for: 5 -> 0; matrix products, arithmetic and copies ran while one was open for 23% -> 0% of each run, Pallas kernels for 0% -> 0%
where the time goes in v1:
time: 63 us; the launch traced here: 62.6 us
  Pallas kernels  54.5 us (87%)
  local copies, waits for them, and re-layouts  7.48 us (12%)
  between operations  0.65 us (1%)
    pallas_call x1, Pallas kernels, fused(): pl.pallas_call(functools.partial(block_kernel, (n_tm, height, width, chan...  54.5 us
    unnamed x13, local copies, waits for them, and re-layouts  7.48 us

profile of v1, /device:TPU:0, one launch (start us, length us, event | category | flops | bytes accessed | tf_op | source)
XLA Modules:
  0.0 62.6 jit_solution(7006004353809618936)
XLA Ops:
  0.6 0.0 copy-start.4
  0.6 0.7 %copy-done.4 = f32[320]{0:T(512)S(1)} copy-done((f32[320]{0:T(512)S(1)}, f32[320]{0:T(512)}, u32[]{:S(2)}) %copy-start.4) | copy-done | bytes 1304
  1.3 0.0 copy-start
  1.3 1.1 %copy-done = f32[1,1,16,32,320]{4,3,2,1,0:T(8,128)S(1)} copy-done((f32[1,1,16,32,320]{4,3,2,1,0:T(8,128)S(1)}, f32[1,1,16,32,320]{4,3,2,1,0:T(8,128)}, u32[]{:S(2)}) %copy-start) | copy-done | bytes 655384
  2.4 0.0 copy-start.1
  2.5 1.1 %copy-done.1 = f32[1,1,16,32,320]{4,3,2,1,0:T(8,128)S(1)} copy-done((f32[1,1,16,32,320]{4,3,2,1,0:T(8,128)S(1)}, f32[1,1,16,32,320]{4,3,2,1,0:T(8,128)}, u32[]{:S(2)}) %copy-start.1) | copy-done | bytes 655384
  3.6 0.0 copy-start.2
  3.6 1.0 %copy-done.2 = bf16[9,80,320]{2,1,0:T(8,128)(2,1)S(1)} copy-done((bf16[9,80,320]{2,1,0:T(8,128)(2,1)S(1)}, bf16[9,80,320]{2,1,0:T(8,128)(2,1)}, u32[]{:S(2)}) %copy-start.2) | copy-done | bytes 460824
  4.6 0.0 copy-start.3
  4.6 1.0 %copy-done.3 = f32[3,80,320]{2,1,0:T(8,128)S(1)} copy-done((f32[3,80,320]{2,1,0:T(8,128)S(1)}, f32[3,80,320]{2,1,0:T(8,128)}, u32[]{:S(2)}) %copy-start.3) | copy-done | bytes 307224
  5.6 54.5 %block.1 = (f32[512,320]{1,0:T(8,128)S(1)}, f32[512,320]{1,0:T(8,128)S(1)}, f32[3,80,320]{2,1,0:T(8,128)S(1)}) custom-call(f32[512,320]{1,0:T(8,128)S(1)} %bitcast.4, bf16[9,80,320]{2,1,0:T(8,128)(2,1)S(1)} %copy-done.2, f32[1,320]{1,0:T(1,128)S(1)} %reshape.22.bias_ref, f32[3,80,320]{2,1,0:T(8,128)S(1)} %copy-done.3, f32[512,320]{1,0:T(8,128)S(1)} %bitcast.5), custom_call_target="tpu_custom_call" | custom-call | tf_op jit(solution)/shard_map/block/pallas_call | solution.py:318
  60.1 0.9 %copy.11 = f32[1,1,16,32,320]{4,3,2,1,0:T(8,128)} copy(f32[1,1,16,32,320]{4,3,2,1,0:T(8,128)S(1)} %bitcast.7) | data formatting | bytes 1310720
  61.0 0.9 %copy.12 = f32[1,1,16,32,320]{4,3,2,1,0:T(8,128)} copy(f32[1,1,16,32,320]{4,3,2,1,0:T(8,128)S(1)} %bitcast.6) | data formatting | bytes 1310720
  61.9 0.7 %copy.13 = f32[3,80,320]{2,1,0:T(8,128)} copy(f32[3,80,320]{2,1,0:T(8,128)S(1)} %get-tuple-element.14) | data formatting | bytes 614400
  (1 shorter events, 0.0 us)
Async XLA Ops:
  0.6 0.7 %copy-start.4 = (f32[320]{0:T(512)S(1)}, f32[320]{0:T(512)}, u32[]{:S(2)}) copy-start(f32[320]{0:T(512)} %param.7) | copy-start | bytes 3844
  1.3 1.1 %copy-start = (f32[1,1,16,32,320]{4,3,2,1,0:T(8,128)S(1)}, f32[1,1,16,32,320]{4,3,2,1,0:T(8,128)}, u32[]{:S(2)}) copy-start(f32[1,1,16,32,320]{4,3,2,1,0:T(8,128)} %param.5) | copy-start | bytes 1966084
  2.4 1.1 %copy-start.1 = (f32[1,1,16,32,320]{4,3,2,1,0:T(8,128)S(1)}, f32[1,1,16,32,320]{4,3,2,1,0:T(8,128)}, u32[]{:S(2)}) copy-start(f32[1,1,16,32,320]{4,3,2,1,0:T(8,128)} %param.9) | copy-start | bytes 1966084
  3.6 1.1 %copy-start.2 = (bf16[9,80,320]{2,1,0:T(8,128)(2,1)S(1)}, bf16[9,80,320]{2,1,0:T(8,128)(2,1)}, u32[]{:S(2)}) copy-start(bf16[9,80,320]{2,1,0:T(8,128)(2,1)} %sw_h.1) | copy-start | bytes 1382404
  4.6 1.0 %copy-start.3 = (f32[3,80,320]{2,1,0:T(8,128)S(1)}, f32[3,80,320]{2,1,0:T(8,128)}, u32[]{:S(2)}) copy-start(f32[3,80,320]{2,1,0:T(8,128)} %tw_h.1) | copy-start | bytes 921604

commit v2 on v1

v2 whole, which is shorter than its diff:
```python
import functools
import math

import jax
import jax.numpy as jnp
from jax import lax
from jax.experimental import pallas as pl
from jax.experimental.pallas import tpu as pltpu
from jax.sharding import PartitionSpec as P

F32 = jnp.float32
BF16 = jnp.bfloat16
MESH = pl.DeviceIdType.MESH


def nn_dot(left, right):
    return lax.dot_general(left, right, (((1,), (0,)), ((), ())), preferred_element_type=F32)


def outer_dot(left, right):
    return lax.dot_general(left, right, (((0,), (0,)), ((), ())), preferred_element_type=F32)


def transpose_dot(left, right):
    return lax.dot_general(left, right, (((1,), (1,)), ((), ())), preferred_element_type=F32)


def block_kernel(
    dims,
    video_h, sw_h, bias_ref, tw_h, cot_h,
    out_v, gv_v, gt_v,
    video, cot, sw, tw, wp, wg, xcat, cb, chalo, hb, hpack, hhalo, slope, gpad,
    gtl, rx, ysend, ry, psum, pb, rs, ag,
    load_sem, w_send, w_recv, halo_send, halo_recv, g_send, g_recv, a_send, a_recv,
):
    n_tm, n_clip, height, width, chans, scale = dims
    rows = height * width
    depth = sw_h.shape[1]
    half = rows // 2
    quarter = rows // 4
    chunks = 4
    chunk = half // chunks
    tm = lax.axis_index("tm")
    c = lax.axis_index("clip")

    def flip(value, bit):
        return value + bit - 2 * bit * (lax.rem(value // bit, 2))

    core, ypart = flip(c, 1), flip(c, 2)
    xpart, zpart = flip(tm, 1), flip(tm, 2)
    parity = lax.rem(tm, 2)
    h = lax.rem(tm // 2, 2)

    barrier = pltpu.get_barrier_semaphore()
    for step in range(1, n_tm):
        pl.semaphore_signal(
            barrier, inc=1, device_id=(lax.rem(tm + step, n_tm), c), device_id_type=MESH
        )
    pl.semaphore_signal(barrier, inc=1, device_id=(tm, core), device_id_type=MESH)
    pl.semaphore_signal(barrier, inc=1, device_id=(tm, ypart), device_id_type=MESH)

    loads = [
        pltpu.make_async_copy(sw_h, sw, load_sem.at[0]),
        pltpu.make_async_copy(tw_h, tw, load_sem.at[1]),
        pltpu.make_async_copy(cot_h, cot, load_sem.at[2]),
        pltpu.make_async_copy(video_h, video, load_sem.at[3]),
    ]
    for load in loads:
        load.start()

    def pack(value):
        return jnp.concatenate([value[:quarter], value[quarter:]], axis=1)

    def unpack(ref, slot):
        parts = []
        for q in range(2):
            both = ref[slot, q * quarter : (q + 1) * quarter]
            parts += [both[:, :chans], both[:, chans:]]
        return jnp.concatenate(parts, axis=0)

    loads[0].wait()
    loads[1].wait()
    shard = [sw[tap] for tap in range(9)] + [tw[tap].astype(BF16) for tap in range(3)]
    for pair in range(6):
        wp[c, pair] = jnp.concatenate([shard[2 * pair], shard[2 * pair + 1]], axis=1)
    pl.semaphore_wait(barrier, n_tm + 1)

    def send(src, dst, ssem, rsem, device):
        copy = pltpu.make_async_remote_copy(
            src_ref=src, dst_ref=dst, send_sem=ssem, recv_sem=rsem,
            device_id=device, device_id_type=MESH,
        )
        copy.start()
        return copy

    def wsend(slot, owner, pair, device):
        part = wp.at[owner, pair]
        return send(part, part, w_send.at[slot], w_recv.at[slot], device)

    y_pairs = [2 * h, 2 * h + 1, 4, 5]
    z_pairs = [2 * (1 - h), 2 * (1 - h) + 1]
    y_copies = [wsend(j, c, y_pairs[j], (tm, ypart)) for j in range(4)]
    own_copy = send(wp.at[c], wp.at[c], w_send.at[6], w_recv.at[6], (tm, core))

    loads[2].wait()
    own_cot = cot[...].astype(BF16)
    for q in range(2):
        cb[q * quarter : (q + 1) * quarter] = pack(own_cot[q * half : (q + 1) * half])

    def near_send(base, own, halo, q):
        part = pl.ds(q * chunk, chunk)
        return send(
            own.at[part, :], halo.at[parity, part, :],
            halo_send.at[base + q], halo_recv.at[base + q], (xpart, c),
        )

    def far_copy(base, halo, q):
        target = lax.rem(tm + n_tm + 2 - 4 * parity, n_tm)
        part = pl.ds(q * chunk, chunk)
        return pltpu.make_async_remote_copy(
            src_ref=halo.at[1 - parity, part, :],
            dst_ref=halo.at[parity, part, :],
            send_sem=halo_send.at[base + chunks + q],
            recv_sem=halo_recv.at[base + chunks + q],
            device_id=(target, c),
            device_id_type=MESH,
        )

    sends_far = jnp.logical_or(
        jnp.logical_and(parity == 0, tm + 2 < n_tm), jnp.logical_and(parity == 1, tm >= 2)
    )
    gets_far = jnp.logical_or(
        jnp.logical_and(parity == 0, tm >= 2), jnp.logical_and(parity == 1, tm + 2 < n_tm)
    )

    def far_start(base, halo, q):
        @pl.when(sends_far)
        def _():
            far_copy(base, halo, q).start()

    def far_recv(base, halo):
        @pl.when(gets_far)
        def _():
            for q in range(chunks):
                far_copy(base, halo, q).wait_recv()

    def far_done(base, halo):
        @pl.when(sends_far)
        def _():
            for q in range(chunks):
                far_copy(base, halo, q).wait_send()

    cot_near = [near_send(0, cb, chalo, q) for q in range(chunks)]

    for edge, slot in ((0, 0), (n_tm - 1, 1)):
        @pl.when(tm == edge)
        def _():
            chalo[slot] = jnp.zeros((half, 2 * chans), BF16)
            hhalo[slot] = jnp.zeros((half, 2 * chans), BF16)

    column = lax.rem(lax.broadcasted_iota(jnp.int32, (rows, chans), 0), width)

    def shifted(value, step):
        if step == 0:
            return value
        rolled = pltpu.roll(value, step % rows, 0)
        return jnp.where(column == (0 if step == 1 else width - 1), 0.0, rolled)

    xcat[0:width] = jnp.zeros((width, 3 * chans), BF16)
    xcat[width + rows :] = jnp.zeros((width, 3 * chans), BF16)
    for b in range(3):
        gpad[b, 0:width] = jnp.zeros((width, chans), BF16)
        gpad[b, width + rows :] = jnp.zeros((width, chans), BF16)
    loads[3].wait()
    frame = video[...]
    xcat[width : width + rows] = jnp.concatenate(
        [shifted(frame, 1).astype(BF16), frame.astype(BF16), shifted(frame, -1).astype(BF16)], axis=1
    )

    relays = []
    z_copies = []
    for j in range(2):
        y_copies[j].wait_recv()
        z_copies.append(wsend(4 + j, ypart, y_pairs[j], (zpart, c)))
        relays.append(wsend(7 + j, ypart, y_pairs[j], (tm, core)))
        for q in (2 * j, 2 * j + 1):
            cot_near[q].wait_recv()
            far_start(0, chalo, q)
    y_copies[2].wait_recv()
    relays.append(wsend(9, ypart, y_pairs[2], (tm, core)))
    for j in range(2):
        z_copies[j].wait_recv()
        relays.append(wsend(11 + j, ypart, z_pairs[j], (tm, core)))
    own_copy.wait_recv()
    for copy in relays:
        copy.wait_recv()

    def unpack_weights(pair):
        for owner in range(n_clip):
            both = wp[owner, pair]
            band = slice(owner * depth, (owner + 1) * depth)
            wg[2 * pair, band] = both[:, :chans]
            wg[2 * pair + 1, band] = both[:, chans:]

    for pair in range(5):
        unpack_weights(pair)

    hid_near = []
    for q in range(2):
        acc = bias_ref[...].reshape(1, chans) + jnp.zeros((half, chans), F32)
        for a in range(3):
            acc = acc + nn_dot(
                xcat[a * width + q * half : a * width + (q + 1) * half],
                wg[3 * a : 3 * a + 3].reshape(3 * chans, chans),
            )
        sig = jax.nn.sigmoid(acc)
        hidden = (acc * sig).astype(BF16)
        hb[q * half : (q + 1) * half] = hidden
        hpack[q * quarter : (q + 1) * quarter] = pack(hidden)
        hid_near += [near_send(2 * chunks, hpack, hhalo, 2 * q + e) for e in range(2)]
        slope[q * half : (q + 1) * half] = sig * (1.0 + acc * (1.0 - sig))

    y_copies[3].wait_recv()
    relays.append(wsend(10, ypart, y_pairs[3], (tm, core)))

    lanes = psum.shape[2]
    far_recv(0, chalo)
    hidden_all = hb[...]
    own_cot = cot[...].astype(BF16)
    before, after = unpack(chalo, 0), unpack(chalo, 1)
    products = jnp.concatenate(
        [outer_dot(hidden_all, right) for right in (after, own_cot, before)]
        + [jnp.zeros((chans, n_tm * lanes - 3 * chans), F32)],
        axis=1,
    )
    for owner in range(n_clip):
        gtl[owner % 2, owner // 2] = products[owner * depth : (owner + 1) * depth]
    core_copy = send(
        gtl.at[1 - lax.rem(c, 2)], rx, g_send.at[0], g_recv.at[0], (tm, core)
    )

    def pass_hidden(q):
        hid_near[q].wait_recv()
        far_start(2 * chunks, hhalo, q)

    relays[-1].wait_recv()
    unpack_weights(5)
    grad_h = transpose_dot(after, wg[9]) + transpose_dot(own_cot, wg[10])
    grad_h = grad_h + transpose_dot(before, wg[11])
    pass_hidden(0)

    core_copy.wait_recv()
    yc = c // 2
    mine = lax.rem(c, 2)
    ysend[...] = (gtl[mine, 1 - yc] + rx[1 - yc]).astype(BF16)
    grad_y = send(ysend, ry, g_send.at[1], g_recv.at[1], (tm, ypart))

    grad_s = grad_h * slope[...]
    for b in range(3):
        gpad[b, width : width + rows] = shifted(grad_s, b - 1).astype(BF16)
    pass_hidden(1)
    pass_hidden(2)

    def grad_conv(q):
        acc = cot[q * half : (q + 1) * half]
        for a in range(3):
            start = (2 - a) * width + q * half
            for b in range(3):
                acc = acc + transpose_dot(gpad[b, start : start + half], wg[3 * a + b])
        gv_v[q * half : (q + 1) * half] = acc

    grad_conv(0)
    pass_hidden(3)

    own_sum = gtl[mine, yc] + rx[yc]
    grad_y.wait_recv()
    own_sum = own_sum + ry[...].astype(F32)
    for to in range(n_tm):
        part = own_sum[:, to * lanes : (to + 1) * lanes]
        psum[to] = part
        pb[to] = part.astype(BF16)
    scatters = []
    for step in range(1, n_tm):
        to = lax.rem(tm + step, n_tm)
        scatters.append(
            send(pb.at[to], rs.at[step - 1], a_send.at[step - 1], a_recv.at[step - 1], (to, c))
        )
    grad_conv(1)
    out_v[...] = video[...] + nn_dot(hb[...], wg[10])

    for copy in scatters:
        copy.wait_recv()
    total = psum[tm]
    for step in range(1, n_tm):
        total = total + rs[step - 1].astype(F32)
    ag[tm] = total.astype(BF16)
    gathers = []
    for step in range(1, n_tm):
        to = lax.rem(tm + step, n_tm)
        slot = n_tm - 2 + step
        gathers.append(send(ag.at[tm], ag.at[tm], a_send.at[slot], a_recv.at[slot], (to, c)))

    far_recv(2 * chunks, hhalo)
    out_v[...] = out_v[...] + nn_dot(unpack(hhalo, 0), wg[9]) + nn_dot(unpack(hhalo, 1), wg[11])

    for copy in gathers:
        copy.wait_recv()
    whole = jnp.concatenate([ag[to] for to in range(n_tm)], axis=1).astype(F32) * scale
    for k in range(3):
        gt_v[k] = whole[:, k * chans : (k + 1) * chans]

    for copy in (
        y_copies + z_copies + [own_copy] + relays + cot_near + hid_near
        + [core_copy, grad_y] + scatters + gathers
    ):
        copy.wait_send()
    far_done(0, chalo)
    far_done(2 * chunks, hhalo)


def fused(n_tm, n_clip, video, spatial_w, spatial_b, temporal_w, cotangent):
    clips, frames, height, width, chans = video.shape
    rows = height * width
    depth = spatial_w.shape[1]
    lanes = -(-3 * chans // (128 * n_tm)) * 128
    scale = 1.0 / math.sqrt(rows * n_tm * n_clip)
    any_spec = pl.BlockSpec(memory_space=pltpu.HBM)
    vm_spec = pl.BlockSpec(memory_space=pltpu.VMEM)
    vm = pltpu.VMEM
    dma = pltpu.SemaphoreType.DMA
    out, gv, gt = pl.pallas_call(
        functools.partial(block_kernel, (n_tm, n_clip, height, width, chans, scale)),
        out_shape=(
            jax.ShapeDtypeStruct((rows, chans), F32),
            jax.ShapeDtypeStruct((rows, chans), F32),
            jax.ShapeDtypeStruct((3, depth, chans), F32),
        ),
        in_specs=[any_spec, any_spec, vm_spec, any_spec, any_spec],
        out_specs=(vm_spec, vm_spec, vm_spec),
        scratch_shapes=[
            vm((rows, chans), F32),
            vm((rows, chans), F32),
            vm((9, depth, chans), BF16),
            vm((3, depth, chans), F32),
            vm((n_clip, 6, depth, 2 * chans), BF16),
            vm((12, chans, chans), BF16),
            vm((rows + 2 * width, 3 * chans), BF16),
            vm((rows // 2, 2 * chans), BF16),
            vm((2, rows // 2, 2 * chans), BF16),
            vm((rows, chans), BF16),
            vm((rows // 2, 2 * chans), BF16),
            vm((2, rows // 2, 2 * chans), BF16),
            vm((rows, chans), F32),
            vm((3, rows + 2 * width, chans), BF16),
            vm((2, 2, depth, n_tm * lanes), F32),
            vm((2, depth, n_tm * lanes), F32),
            vm((depth, n_tm * lanes), BF16),
            vm((depth, n_tm * lanes), BF16),
            vm((n_tm, depth, lanes), F32),
            vm((n_tm, depth, lanes), BF16),
            vm((n_tm - 1, depth, lanes), BF16),
            vm((n_tm, depth, lanes), BF16),
            dma((4,)),
            dma((13,)),
            dma((13,)),
            dma((16,)),
            dma((16,)),
            dma((2,)),
            dma((2,)),
            dma((2 * n_tm - 2,)),
            dma((2 * n_tm - 2,)),
        ],
        compiler_params=pltpu.CompilerParams(
            collective_id=0, has_side_effects=True, vmem_limit_bytes=40 * 2**20
        ),
        name="block",
    )(
        video.reshape(rows, chans), spatial_w, spatial_b, temporal_w,
        cotangent.reshape(rows, chans),
    )
    return out.reshape(video.shape), gv.reshape(video.shape), gt


def padded_2(cells, sides, width):
    for axis, dim in sides:
        count = lax.axis_size(axis)
        ends = count - 1
        head = lax.slice_in_dim(cells, 0, width, axis=dim)
        tail = lax.slice_in_dim(cells, cells.shape[dim] - width, cells.shape[dim], axis=dim)
        cells = jnp.concatenate(
            [
                lax.ppermute(tail, axis, [(i, (i + 1) % count) for i in range(ends)]),
                cells,
                lax.ppermute(head, axis, [((i + 1) % count, i) for i in range(ends)]),
            ],
            axis=dim,
        )
    return cells


def native(video, spatial_w, spatial_b, temporal_w, cotangent):
    clips, frames, height, width, chans = video.shape
    row_count = clips * frames * height * width
    pads = ((0, 0), (0, 0), (1, 1), (1, 1), (0, 0))
    padded = jnp.pad(video.astype(BF16), pads)
    temporal_b = temporal_w.astype(BF16)
    spatial_all = lax.all_gather(spatial_w, "clip", axis=1, tiled=True)
    temporal_all = lax.all_gather(temporal_b, "clip", axis=1, tiled=True)
    spatial = jnp.zeros((row_count, chans), F32)
    for y in range(3):
        for x in range(3):
            window = padded[:, :, y : y + height, x : x + width, :].reshape(row_count, chans)
            spatial = spatial + nn_dot(window, spatial_all[3 * y + x])
    spatial = spatial + spatial_b
    sigmoid_s = jax.nn.sigmoid(spatial)
    hidden = (spatial * sigmoid_s).astype(BF16).reshape(video.shape)
    hidden_pad = padded_2(hidden, (("tm", 1),), 1)
    cot_b = cotangent.astype(BF16)
    cot_flat = cot_b.reshape(row_count, chans)
    cot_pad = padded_2(cot_b, (("tm", 1),), 1)
    temporal = jnp.zeros((row_count, chans), F32)
    grad_hidden = jnp.zeros((row_count, chans), F32)
    grads = []
    for k in range(3):
        shifted_hid = hidden_pad[:, k : k + frames].reshape(row_count, chans)
        temporal = temporal + nn_dot(shifted_hid, temporal_all[k])
        shifted_cot = cot_pad[:, 2 - k : 2 - k + frames].reshape(row_count, chans)
        grad_hidden = grad_hidden + transpose_dot(shifted_cot, temporal_all[k])
        grads.append(outer_dot(shifted_hid, cot_flat))
    total_rows = row_count * lax.axis_size("tm") * lax.axis_size("clip")
    summed = lax.psum(jnp.stack(grads), "tm")
    owned = lax.psum_scatter(summed, "clip", scatter_dimension=1, tiled=True)
    grad_spatial = (grad_hidden * sigmoid_s * (1.0 + spatial * (1.0 - sigmoid_s))).astype(BF16)
    grad_frames = jnp.pad(grad_spatial.reshape(video.shape), pads)
    grad_acc = cotangent.reshape(row_count, chans)
    for y in range(3):
        for x in range(3):
            window = grad_frames[:, :, 2 - y : 2 - y + height, 2 - x : 2 - x + width, :]
            window = window.reshape(row_count, chans)
            grad_acc = grad_acc + transpose_dot(window, spatial_all[3 * y + x])
    return (
        video + temporal.reshape(video.shape),
        grad_acc.reshape(video.shape),
        owned * (1.0 / math.sqrt(total_rows)),
    )


def solution(mesh):
    n_tm, n_clip = mesh.shape["tm"], mesh.shape["clip"]

    def on_device(video, spatial_w, spatial_b, temporal_w, cotangent):
        args = (video, spatial_w, spatial_b, temporal_w, cotangent)
        one_frame = video.shape[0] == 1 and video.shape[1] == 1
        if one_frame and spatial_w.shape[1] % 16 == 0 and n_clip == 4 and n_tm % 4 == 0:
            return fused(n_tm, n_clip, *args)
        return native(*args)

    return jax.shard_map(
        on_device,
        mesh=mesh,
        in_specs=(
            P("clip", "tm", None, None, None),
            P(None, "clip", None),
            P(),
            P(None, "clip", None),
            P("clip", "tm", None, None, None),
        ),
        out_specs=(
            P("clip", "tm", None, None, None),
            P("clip", "tm", None, None, None),
            P(None, "clip", None),
        ),
        check_vma=False,
    )
```

time: 63 us -> 53.1 us (0.84)
  Pallas kernels: 54.5 us -> 44.7 us
    pallas_call x1, Pallas kernels: 54.5 us -> 44.7 us  [fused(): pl.pallas_call(functools.partial(block_kernel, (n_tm, n_clip, height, wid...]
where the time goes in v2:
time: 53.1 us; the launch traced here: 52.8 us
  Pallas kernels  44.7 us (84%)
  local copies, waits for them, and re-layouts  7.48 us (14%)
  between operations  0.65 us (1%)
    pallas_call x1, Pallas kernels, fused(): pl.pallas_call(functools.partial(block_kernel, (n_tm, n_clip, height, wid...  44.7 us
    unnamed x13, local copies, waits for them, and re-layouts  7.48 us

profile of v2, /device:TPU:0, one launch (start us, length us, event | category | flops | bytes accessed | tf_op | source)
XLA Modules:
  0.0 52.8 jit_solution(447763305035512164)
XLA Ops:
  0.6 0.0 copy-start.4
  0.6 0.7 %copy-done.4 = f32[320]{0:T(512)S(1)} copy-done((f32[320]{0:T(512)S(1)}, f32[320]{0:T(512)}, u32[]{:S(2)}) %copy-start.4) | copy-done | bytes 1304
  1.3 0.0 copy-start
  1.3 1.1 %copy-done = f32[1,1,16,32,320]{4,3,2,1,0:T(8,128)S(1)} copy-done((f32[1,1,16,32,320]{4,3,2,1,0:T(8,128)S(1)}, f32[1,1,16,32,320]{4,3,2,1,0:T(8,128)}, u32[]{:S(2)}) %copy-start) | copy-done | bytes 655384
  2.4 0.0 copy-start.1
  2.5 1.1 %copy-done.1 = f32[1,1,16,32,320]{4,3,2,1,0:T(8,128)S(1)} copy-done((f32[1,1,16,32,320]{4,3,2,1,0:T(8,128)S(1)}, f32[1,1,16,32,320]{4,3,2,1,0:T(8,128)}, u32[]{:S(2)}) %copy-start.1) | copy-done | bytes 655384
  3.6 0.0 copy-start.2
  3.6 1.0 %copy-done.2 = bf16[9,80,320]{2,1,0:T(8,128)(2,1)S(1)} copy-done((bf16[9,80,320]{2,1,0:T(8,128)(2,1)S(1)}, bf16[9,80,320]{2,1,0:T(8,128)(2,1)}, u32[]{:S(2)}) %copy-start.2) | copy-done | bytes 460824
  4.6 0.0 copy-start.3
  4.6 1.0 %copy-done.3 = f32[3,80,320]{2,1,0:T(8,128)S(1)} copy-done((f32[3,80,320]{2,1,0:T(8,128)S(1)}, f32[3,80,320]{2,1,0:T(8,128)}, u32[]{:S(2)}) %copy-start.3) | copy-done | bytes 307224
  5.6 44.7 %block.1 = (f32[512,320]{1,0:T(8,128)S(1)}, f32[512,320]{1,0:T(8,128)S(1)}, f32[3,80,320]{2,1,0:T(8,128)S(1)}) custom-call(f32[512,320]{1,0:T(8,128)S(1)} %bitcast.6, bf16[9,80,320]{2,1,0:T(8,128)(2,1)S(1)} %copy-done.2, f32[320]{0:T(512)S(1)} %copy-done.4, f32[3,80,320]{2,1,0:T(8,128)S(1)} %copy-done.3, f32[512,320]{1,0:T(8,128)S(1)} %bitcast.7), custom_call_target="tpu_custom_call" | custom-call | tf_op jit(solution)/shard_map/block/pallas_call | solution.py:331
  50.3 0.9 %copy.11 = f32[1,1,16,32,320]{4,3,2,1,0:T(8,128)} copy(f32[1,1,16,32,320]{4,3,2,1,0:T(8,128)S(1)} %bitcast.5) | data formatting | bytes 1310720
  51.2 0.9 %copy.12 = f32[1,1,16,32,320]{4,3,2,1,0:T(8,128)} copy(f32[1,1,16,32,320]{4,3,2,1,0:T(8,128)S(1)} %bitcast.4) | data formatting | bytes 1310720
  52.1 0.7 %copy.13 = f32[3,80,320]{2,1,0:T(8,128)} copy(f32[3,80,320]{2,1,0:T(8,128)S(1)} %get-tuple-element.14) | data formatting | bytes 614400
Async XLA Ops:
  0.6 0.7 %copy-start.4 = (f32[320]{0:T(512)S(1)}, f32[320]{0:T(512)}, u32[]{:S(2)}) copy-start(f32[320]{0:T(512)} %bias_ref.1) | copy-start | bytes 3844
  1.3 1.1 %copy-start = (f32[1,1,16,32,320]{4,3,2,1,0:T(8,128)S(1)}, f32[1,1,16,32,320]{4,3,2,1,0:T(8,128)}, u32[]{:S(2)}) copy-start(f32[1,1,16,32,320]{4,3,2,1,0:T(8,128)} %param.5) | copy-start | bytes 1966084
  2.4 1.1 %copy-start.1 = (f32[1,1,16,32,320]{4,3,2,1,0:T(8,128)S(1)}, f32[1,1,16,32,320]{4,3,2,1,0:T(8,128)}, u32[]{:S(2)}) copy-start(f32[1,1,16,32,320]{4,3,2,1,0:T(8,128)} %param.9) | copy-start | bytes 1966084
  3.6 1.1 %copy-start.2 = (bf16[9,80,320]{2,1,0:T(8,128)(2,1)S(1)}, bf16[9,80,320]{2,1,0:T(8,128)(2,1)}, u32[]{:S(2)}) copy-start(bf16[9,80,320]{2,1,0:T(8,128)(2,1)} %sw_h.1) | copy-start | bytes 1382404
  4.6 1.0 %copy-start.3 = (f32[3,80,320]{2,1,0:T(8,128)S(1)}, f32[3,80,320]{2,1,0:T(8,128)}, u32[]{:S(2)}) copy-start(f32[3,80,320]{2,1,0:T(8,128)} %tw_h.1) | copy-start | bytes 921604

commit v3 on v2

--- a/solution.py
+++ b/solution.py
@@ -28,10 +28,10 @@
 def block_kernel(
     dims,
     video_h, sw_h, bias_ref, tw_h, cot_h,
-    out_v, gv_v, gt_v,
+    out_h, gv_h, gt_h,
     video, cot, sw, tw, wp, wg, xcat, cb, chalo, hb, hpack, hhalo, slope, gpad,
-    gtl, rx, ysend, ry, psum, pb, rs, ag,
-    load_sem, w_send, w_recv, halo_send, halo_recv, g_send, g_recv, a_send, a_recv,
+    out_v, gv_v, gt_v, gtl, rx, ysend, ry, psum, pb, rs, ag,
+    load_sem, out_sem, w_send, w_recv, halo_send, halo_recv, g_send, g_recv, a_send, a_recv,
 ):
     n_tm, n_clip, height, width, chans, scale = dims
     rows = height * width
@@ -235,9 +235,12 @@
     )
     for owner in range(n_clip):
         gtl[owner % 2, owner // 2] = products[owner * depth : (owner + 1) * depth]
-    core_copy = send(
-        gtl.at[1 - lax.rem(c, 2)], rx, g_send.at[0], g_recv.at[0], (tm, core)
-    )
+    yc = c // 2
+    mine = lax.rem(c, 2)
+    core_copies = [
+        send(gtl.at[1 - mine, side], rx.at[side], g_send.at[e], g_recv.at[e], (tm, core))
+        for e, side in enumerate((1 - yc, yc))
+    ]
 
     def pass_hidden(q):
         hid_near[q].wait_recv()
@@ -249,11 +252,9 @@
     grad_h = grad_h + transpose_dot(before, wg[11])
     pass_hidden(0)
 
-    core_copy.wait_recv()
-    yc = c // 2
-    mine = lax.rem(c, 2)
+    core_copies[0].wait_recv()
     ysend[...] = (gtl[mine, 1 - yc] + rx[1 - yc]).astype(BF16)
-    grad_y = send(ysend, ry, g_send.at[1], g_recv.at[1], (tm, ypart))
+    grad_y = send(ysend, ry, g_send.at[2], g_recv.at[2], (tm, ypart))
 
     grad_s = grad_h * slope[...]
     for b in range(3):
@@ -272,6 +273,7 @@
     grad_conv(0)
     pass_hidden(3)
 
+    core_copies[1].wait_recv()
     own_sum = gtl[mine, yc] + rx[yc]
     grad_y.wait_recv()
     own_sum = own_sum + ry[...].astype(F32)
@@ -279,13 +281,16 @@
         part = own_sum[:, to * lanes : (to + 1) * lanes]
         psum[to] = part
         pb[to] = part.astype(BF16)
+    order = sorted(range(1, n_tm), key=lambda step: -min(step, n_tm - step))
     scatters = []
-    for step in range(1, n_tm):
+    for step in order:
         to = lax.rem(tm + step, n_tm)
         scatters.append(
             send(pb.at[to], rs.at[step - 1], a_send.at[step - 1], a_recv.at[step - 1], (to, c))
         )
     grad_conv(1)
+    gv_out = pltpu.make_async_copy(gv_v, gv_h, out_sem.at[0])
+    gv_out.start()
     out_v[...] = video[...] + nn_dot(hb[...], wg[10])
 
     for copy in scatters:
@@ -295,27 +300,48 @@
         total = total + rs[step - 1].astype(F32)
     ag[tm] = total.astype(BF16)
     gathers = []
-    for step in range(1, n_tm):
+    for step in order:
         to = lax.rem(tm + step, n_tm)
         slot = n_tm - 2 + step
         gathers.append(send(ag.at[tm], ag.at[tm], a_send.at[slot], a_recv.at[slot], (to, c)))
 
     far_recv(2 * chunks, hhalo)
     out_v[...] = out_v[...] + nn_dot(unpack(hhalo, 0), wg[9]) + nn_dot(unpack(hhalo, 1), wg[11])
+    out_out = pltpu.make_async_copy(out_v, out_h, out_sem.at[1])
+    out_out.start()
 
     for copy in gathers:
         copy.wait_recv()
     whole = jnp.concatenate([ag[to] for to in range(n_tm)], axis=1).astype(F32) * scale
     for k in range(3):
         gt_v[k] = whole[:, k * chans : (k + 1) * chans]
+    gt_out = pltpu.make_async_copy(gt_v, gt_h, out_sem.at[2])
+    gt_out.start()
 
     for copy in (
         y_copies + z_copies + [own_copy] + relays + cot_near + hid_near
-        + [core_copy, grad_y] + scatters + gathers
+        + core_copies + [grad_y] + scatters + gathers
     ):
         copy.wait_send()
     far_done(0, chalo)
     far_done(2 * chunks, hhalo)
+    gv_out.wait()
+    out_out.wait()
+    gt_out.wait()
+
+
+def hand_over(*refs):
+    n = (len(refs) - 2) // 3
+    ins, outs, held, (sem_in, sem_out) = refs[:n], refs[n : 2 * n], refs[2 * n : 3 * n], refs[3 * n :]
+    reads = [pltpu.make_async_copy(ins[e], held[e], sem_in.at[e]) for e in range(n)]
+    writes = [pltpu.make_async_copy(held[e], outs[e], sem_out.at[e]) for e in range(n)]
+    for read in reads:
+        read.start()
+    for read, write in zip(reads, writes):
+        read.wait()
+        write.start()
+    for write in writes:
+        write.wait()
 
 
 def fused(n_tm, n_clip, video, spatial_w, spatial_b, temporal_w, cotangent):
@@ -328,7 +354,7 @@
     vm_spec = pl.BlockSpec(memory_space=pltpu.VMEM)
     vm = pltpu.VMEM
     dma = pltpu.SemaphoreType.DMA
-    out, gv, gt = pl.pallas_call(
+    results = pl.pallas_call(
         functools.partial(block_kernel, (n_tm, n_clip, height, width, chans, scale)),
         out_shape=(
             jax.ShapeDtypeStruct((rows, chans), F32),
@@ -336,7 +362,7 @@
             jax.ShapeDtypeStruct((3, depth, chans), F32),
         ),
         in_specs=[any_spec, any_spec, vm_spec, any_spec, any_spec],
-        out_specs=(vm_spec, vm_spec, vm_spec),
+        out_specs=(any_spec, any_spec, any_spec),
         scratch_shapes=[
             vm((rows, chans), F32),
             vm((rows, chans), F32),
@@ -352,6 +378,9 @@
             vm((2, rows // 2, 2 * chans), BF16),
             vm((rows, chans), F32),
             vm((3, rows + 2 * width, chans), BF16),
+            vm((rows, chans), F32),
+            vm((rows, chans), F32),
+            vm((3, depth, chans), F32),
             vm((2, 2, depth, n_tm * lanes), F32),
             vm((2, depth, n_tm * lanes), F32),
             vm((depth, n_tm * lanes), BF16),
@@ -361,23 +390,34 @@
             vm((n_tm - 1, depth, lanes), BF16),
             vm((n_tm, depth, lanes), BF16),
             dma((4,)),
+            dma((3,)),
             dma((13,)),
             dma((13,)),
             dma((16,)),
             dma((16,)),
-            dma((2,)),
-            dma((2,)),
+            dma((3,)),
+            dma((3,)),
             dma((2 * n_tm - 2,)),
             dma((2 * n_tm - 2,)),
         ],
         compiler_params=pltpu.CompilerParams(
-            collective_id=0, has_side_effects=True, vmem_limit_bytes=40 * 2**20
+            collective_id=0, has_side_effects=True, vmem_limit_bytes=62 * 2**20
         ),
         name="block",
     )(
         video.reshape(rows, chans), spatial_w, spatial_b, temporal_w,
         cotangent.reshape(rows, chans),
     )
+    shapes = tuple(jax.ShapeDtypeStruct(array.shape, F32) for array in results)
+    out, gv, gt = pl.pallas_call(
+        hand_over,
+        out_shape=shapes,
+        in_specs=[any_spec] * 3,
+        out_specs=(any_spec,) * 3,
+        scratch_shapes=[vm(shape.shape, F32) for shape in shapes] + [dma((3,)), dma((3,))],
+        compiler_params=pltpu.CompilerParams(vmem_limit_bytes=62 * 2**20),
+        name="hand_over",
+    )(*results)
     return out.reshape(video.shape), gv.reshape(video.shape), gt
 
 

time: 53.1 us -> 50.1 us (0.944)
  local copies, waits for them, and re-layouts: 7.48 us -> 0 us
  Pallas kernels: 44.7 us -> 49.3 us
    unnamed x13 -> x0, local copies, waits for them, and re-layouts: 7.48 us -> none
    pallas_call x0 -> x1, Pallas kernels: none -> 2.44 us  [fused(): pl.pallas_call(hand_over, out_shape=shapes, in_specs=[any_spec] * 3, out_...]
    pallas_call x1, Pallas kernels: 44.7 us -> 46.8 us  [fused(): pl.pallas_call(functools.partial(block_kernel, (n_tm, n_clip, height, wid...]
where the time goes in v3:
time: 50.1 us; the launch traced here: 49.9 us
  Pallas kernels  49.3 us (98%)
  between operations  0.64 us (1%)
    pallas_call x1, Pallas kernels, fused(): pl.pallas_call(functools.partial(block_kernel, (n_tm, n_clip, height, wid...  46.8 us
    pallas_call x1, Pallas kernels, fused(): pl.pallas_call(hand_over, out_shape=shapes, in_specs=[any_spec] * 3, out_...  2.44 us

profile of v3, /device:TPU:0, one launch (start us, length us, event | category | flops | bytes accessed | tf_op | source)
XLA Modules:
  0.0 49.9 jit_solution(14981932795518213034)
XLA Ops:
  0.6 46.8 %block.1 = (f32[512,320]{1,0:T(8,128)}, f32[512,320]{1,0:T(8,128)}, f32[3,80,320]{2,1,0:T(8,128)}) custom-call(f32[512,320]{1,0:T(8,128)} %bitcast.4, bf16[9,80,320]{2,1,0:T(8,128)(2,1)} %sw_h.1, f32[320]{0:T(512)} %bias_ref.1, f32[3,80,320]{2,1,0:T(8,128)} %tw_h.1, f32[512,320]{1,0:T(8,128)} %bitcast.5), custom_call_target="tpu_custom_call" | custom-call | tf_op jit(solution)/shard_map/block/pallas_call | solution.py:357
  47.5 2.4 %hand_over.1 = (f32[512,320]{1,0:T(8,128)}, f32[512,320]{1,0:T(8,128)}, f32[3,80,320]{2,1,0:T(8,128)}) custom-call(f32[512,320]{1,0:T(8,128)} %get-tuple-element.9.refs_0_, f32[512,320]{1,0:T(8,128)} %get-tuple-element.10.refs_1_, f32[3,80,320]{2,1,0:T(8,128)} %get-tuple-element.11.refs_2_), custom_call_target="tpu_custom_call" | custom-call | tf_op jit(solution)/shard_map/hand_over/pallas_call | solution.py:412

commit v4 on v3

--- a/solution.py
+++ b/solution.py
@@ -97,8 +97,9 @@
         part = wp.at[owner, pair]
         return send(part, part, w_send.at[slot], w_recv.at[slot], device)
 
-    y_pairs = [2 * h, 2 * h + 1, 4, 5]
-    z_pairs = [2 * (1 - h), 2 * (1 - h) + 1]
+    y_pairs = [parity, 2 + h, 4, 5]
+    shared_pairs = [1 - parity, 3 - h]
+    sharers = [(xpart, c), (zpart, c)]
     y_copies = [wsend(j, c, y_pairs[j], (tm, ypart)) for j in range(4)]
     own_copy = send(wp.at[c], wp.at[c], w_send.at[6], w_recv.at[6], (tm, core))
 
@@ -150,7 +151,7 @@
             for q in range(chunks):
                 far_copy(base, halo, q).wait_send()
 
-    cot_near = [near_send(0, cb, chalo, q) for q in range(chunks)]
+    cot_near = [near_send(0, cb, chalo, q) for q in range(2)]
 
     for edge, slot in ((0, 0), (n_tm - 1, 1)):
         @pl.when(tm == edge)
@@ -181,16 +182,19 @@
     z_copies = []
     for j in range(2):
         y_copies[j].wait_recv()
-        z_copies.append(wsend(4 + j, ypart, y_pairs[j], (zpart, c)))
+        z_copies.append(wsend(4 + j, ypart, y_pairs[j], sharers[j]))
+        if j == 0:
+            cot_near += [near_send(0, cb, chalo, q) for q in range(2, chunks)]
         relays.append(wsend(7 + j, ypart, y_pairs[j], (tm, core)))
-        for q in (2 * j, 2 * j + 1):
-            cot_near[q].wait_recv()
-            far_start(0, chalo, q)
+        cot_near[j].wait_recv()
+        far_start(0, chalo, j)
     y_copies[2].wait_recv()
     relays.append(wsend(9, ypart, y_pairs[2], (tm, core)))
     for j in range(2):
         z_copies[j].wait_recv()
-        relays.append(wsend(11 + j, ypart, z_pairs[j], (tm, core)))
+        relays.append(wsend(11 + j, ypart, shared_pairs[j], (tm, core)))
+        cot_near[2 + j].wait_recv()
+        far_start(0, chalo, 2 + j)
     own_copy.wait_recv()
     for copy in relays:
         copy.wait_recv()
@@ -224,6 +228,7 @@
     relays.append(wsend(10, ypart, y_pairs[3], (tm, core)))
 
     lanes = psum.shape[2]
+    wide = n_tm // 2 * lanes
     far_recv(0, chalo)
     hidden_all = hb[...]
     own_cot = cot[...].astype(BF16)
@@ -253,8 +258,11 @@
     pass_hidden(0)
 
     core_copies[0].wait_recv()
-    ysend[...] = (gtl[mine, 1 - yc] + rx[1 - yc]).astype(BF16)
-    grad_y = send(ysend, ry, g_send.at[2], g_recv.at[2], (tm, ypart))
+    y_sum = (gtl[mine, 1 - yc] + rx[1 - yc]).astype(BF16)
+    grad_y = []
+    for e in range(2):
+        ysend[e] = y_sum[:, e * wide : (e + 1) * wide]
+        grad_y.append(send(ysend.at[e], ry.at[e], g_send.at[2 + e], g_recv.at[2 + e], (tm, ypart)))
 
     grad_s = grad_h * slope[...]
     for b in range(3):
@@ -275,34 +283,50 @@
 
     core_copies[1].wait_recv()
     own_sum = gtl[mine, yc] + rx[yc]
-    grad_y.wait_recv()
-    own_sum = own_sum + ry[...].astype(F32)
-    for to in range(n_tm):
-        part = own_sum[:, to * lanes : (to + 1) * lanes]
-        psum[to] = part
-        pb[to] = part.astype(BF16)
-    order = sorted(range(1, n_tm), key=lambda step: -min(step, n_tm - step))
-    scatters = []
-    for step in order:
-        to = lax.rem(tm + step, n_tm)
-        scatters.append(
-            send(pb.at[to], rs.at[step - 1], a_send.at[step - 1], a_recv.at[step - 1], (to, c))
-        )
+    def scatter_copy(to):
+        return pltpu.make_async_remote_copy(
+            src_ref=pb.at[to], dst_ref=rs.at[tm], send_sem=a_send.at[to], recv_sem=a_recv.at[tm],
+            device_id=(to, c), device_id_type=MESH,
+        )
+
+    def arrival(sender):
+        return pltpu.make_async_remote_copy(
+            src_ref=pb.at[sender], dst_ref=rs.at[sender], send_sem=a_send.at[sender],
+            recv_sem=a_recv.at[sender], device_id=(sender, c), device_id_type=MESH,
+        )
+
+    for e in range(2):
+        grad_y[e].wait_recv()
+        both = own_sum[:, e * wide : (e + 1) * wide] + ry[e].astype(F32)
+        for place in range(n_tm // 2):
+            to = e * (n_tm // 2) + place
+            part = both[:, place * lanes : (place + 1) * lanes]
+            psum[to] = part
+            pb[to] = part.astype(BF16)
+
+            @pl.when(tm != to)
+            def _():
+                scatter_copy(to).start()
+
     grad_conv(1)
     gv_out = pltpu.make_async_copy(gv_v, gv_h, out_sem.at[0])
     gv_out.start()
     out_v[...] = video[...] + nn_dot(hb[...], wg[10])
 
-    for copy in scatters:
-        copy.wait_recv()
+    rs[tm] = jnp.zeros(rs.shape[1:], BF16)
+    for sender in range(n_tm):
+        @pl.when(tm != sender)
+        def _():
+            arrival(sender).wait_recv()
     total = psum[tm]
-    for step in range(1, n_tm):
-        total = total + rs[step - 1].astype(F32)
+    for sender in range(n_tm):
+        total = total + rs[sender].astype(F32)
     ag[tm] = total.astype(BF16)
+    order = sorted(range(1, n_tm), key=lambda step: -min(step, n_tm - step))
     gathers = []
     for step in order:
         to = lax.rem(tm + step, n_tm)
-        slot = n_tm - 2 + step
+        slot = n_tm - 1 + step
         gathers.append(send(ag.at[tm], ag.at[tm], a_send.at[slot], a_recv.at[slot], (to, c)))
 
     far_recv(2 * chunks, hhalo)
@@ -320,11 +344,15 @@
 
     for copy in (
         y_copies + z_copies + [own_copy] + relays + cot_near + hid_near
-        + core_copies + [grad_y] + scatters + gathers
+        + core_copies + grad_y + gathers
     ):
         copy.wait_send()
     far_done(0, chalo)
     far_done(2 * chunks, hhalo)
+    for to in range(n_tm):
+        @pl.when(tm != to)
+        def _():
+            arrival(to).wait_send()
     gv_out.wait()
     out_out.wait()
     gt_out.wait()
@@ -333,8 +361,15 @@
 def hand_over(*refs):
     n = (len(refs) - 2) // 3
     ins, outs, held, (sem_in, sem_out) = refs[:n], refs[n : 2 * n], refs[2 * n : 3 * n], refs[3 * n :]
-    reads = [pltpu.make_async_copy(ins[e], held[e], sem_in.at[e]) for e in range(n)]
-    writes = [pltpu.make_async_copy(held[e], outs[e], sem_out.at[e]) for e in range(n)]
+    reads, writes = [], []
+    for e in range(n):
+        extent = ins[e].shape[0]
+        count = 4 if extent % 64 == 0 else 1
+        for q in range(count):
+            part = pl.ds(q * (extent // count), extent // count)
+            slot = 4 * e + q
+            reads.append(pltpu.make_async_copy(ins[e].at[part], held[e].at[part], sem_in.at[slot]))
+            writes.append(pltpu.make_async_copy(held[e].at[part], outs[e].at[part], sem_out.at[slot]))
     for read in reads:
         read.start()
     for read, write in zip(reads, writes):
@@ -383,11 +418,11 @@
             vm((3, depth, chans), F32),
             vm((2, 2, depth, n_tm * lanes), F32),
             vm((2, depth, n_tm * lanes), F32),
-            vm((depth, n_tm * lanes), BF16),
-            vm((depth, n_tm * lanes), BF16),
+            vm((2, depth, n_tm // 2 * lanes), BF16),
+            vm((2, depth, n_tm // 2 * lanes), BF16),
             vm((n_tm, depth, lanes), F32),
             vm((n_tm, depth, lanes), BF16),
-            vm((n_tm - 1, depth, lanes), BF16),
+            vm((n_tm, depth, lanes), BF16),
             vm((n_tm, depth, lanes), BF16),
             dma((4,)),
             dma((3,)),
@@ -395,10 +430,10 @@
             dma((13,)),
             dma((16,)),
             dma((16,)),
-            dma((3,)),
-            dma((3,)),
-            dma((2 * n_tm - 2,)),
-            dma((2 * n_tm - 2,)),
+            dma((4,)),
+            dma((4,)),
+            dma((2 * n_tm,)),
+            dma((2 * n_tm,)),
         ],
         compiler_params=pltpu.CompilerParams(
             collective_id=0, has_side_effects=True, vmem_limit_bytes=62 * 2**20
@@ -414,7 +449,7 @@
         out_shape=shapes,
         in_specs=[any_spec] * 3,
         out_specs=(any_spec,) * 3,
-        scratch_shapes=[vm(shape.shape, F32) for shape in shapes] + [dma((3,)), dma((3,))],
+        scratch_shapes=[vm(shape.shape, F32) for shape in shapes] + [dma((12,)), dma((12,))],
         compiler_params=pltpu.CompilerParams(vmem_limit_bytes=62 * 2**20),
         name="hand_over",
     )(*results)

time: 50.1 us -> 48 us (0.958)
  Pallas kernels: 49.3 us -> 47.2 us
    pallas_call x1, Pallas kernels: 46.8 us -> 44.6 us  [fused(): pl.pallas_call(functools.partial(block_kernel, (n_tm, n_clip, height, wid...]
where the time goes in v4:
time: 48 us; the launch traced here: 47.8 us
  Pallas kernels  47.2 us (98%)
  between operations  0.64 us (1%)
    pallas_call x1, Pallas kernels, fused(): pl.pallas_call(functools.partial(block_kernel, (n_tm, n_clip, height, wid...  44.6 us
    pallas_call x1, Pallas kernels, fused(): pl.pallas_call(hand_over, out_shape=shapes, in_specs=[any_spec] * 3, out_...  2.53 us

profile of v4, /device:TPU:0, one launch (start us, length us, event | category | flops | bytes accessed | tf_op | source)
XLA Modules:
  0.0 47.8 jit_solution(17540960912105228908)
XLA Ops:
  0.6 44.6 %block.1 = (f32[512,320]{1,0:T(8,128)}, f32[512,320]{1,0:T(8,128)}, f32[3,80,320]{2,1,0:T(8,128)}) custom-call(f32[512,320]{1,0:T(8,128)} %bitcast.4, bf16[9,80,320]{2,1,0:T(8,128)(2,1)} %sw_h.1, f32[320]{0:T(512)} %bias_ref.1, f32[3,80,320]{2,1,0:T(8,128)} %tw_h.1, f32[512,320]{1,0:T(8,128)} %bitcast.5), custom_call_target="tpu_custom_call" | custom-call | tf_op jit(solution)/shard_map/block/pallas_call | solution.py:392
  45.3 2.5 %hand_over.1 = (f32[512,320]{1,0:T(8,128)}, f32[512,320]{1,0:T(8,128)}, f32[3,80,320]{2,1,0:T(8,128)}) custom-call(f32[512,320]{1,0:T(8,128)} %get-tuple-element.9.refs_0_, f32[512,320]{1,0:T(8,128)} %get-tuple-element.10.refs_1_, f32[3,80,320]{2,1,0:T(8,128)} %get-tuple-element.11.refs_2_), custom_call_target="tpu_custom_call" | custom-call | tf_op jit(solution)/shard_map/hand_over/pallas_call | solution.py:447
